TPU v7x, 32 devices: a whole 2x2x4 slice. The times are simulated.
32 devices in a mesh: pipe: 1, expert: 32 (over z, y, x, core).
Axes of the slice: x: 2, y: 2, z: 4, core: 2. Of those that a mesh axis runs over, the one named last changes fastest.
Arguments:
- inputs: bfloat16 [1, 2, 2048, 2048], P('pipe', None, 'expert'), may hold values from -6 to 6
- grads_out: bfloat16 [1, 2, 2048, 2048], P('pipe', None, 'expert'), may hold values from -6 to 6
- expert_ids: int32 [1, 2, 2048, 6], P('pipe', None, 'expert'), may hold values from 0 to 31, all different within a row; in each aligned block of 64 rows (0 to 63, 64 to 127, ..., all dimensions but the last counted through in order) at most 32 rows name the same one
- gate_values: float32 [1, 2, 2048, 6], P('pipe', None, 'expert'), may hold values from 0.1 to 0.5
- w_gate: bfloat16 [1, 32, 2048, 768], P('pipe', 'expert'), may hold values from -0.125 to 0.125
- w_up: bfloat16 [1, 32, 2048, 768], P('pipe', 'expert'), may hold values from -0.125 to 0.125
- w_down: bfloat16 [1, 32, 768, 2048], P('pipe', 'expert'), may hold values from -0.21875 to 0.21875
Outputs:
- received: bfloat16 [1, 2, 2048, 2048], P('pipe', None, 'expert')
- gate_grad: float32 [1, 2, 2048, 6], P('pipe', None, 'expert')
Inputs may be any that keep to these rules, and one draw needn't show every extreme that they name: `expert_ids`: each row names 6 different experts. Within the 64 rows of one device for one section and micro-batch, no expert is named by more than 32 rows, a bound that some expert reaches in some of these blocks.
All inputs are finite; a program needn't handle non-finite values.
Results may differ from a plain program's by a relative error of at most 0.0041.
Values may be sent and summed in bfloat16 or wider, within the bound.
A program may use at most 128 MiB of HBM per device.

v0:
```python
import jax
import jax.numpy as jnp
from jax import lax
from jax.sharding import PartitionSpec as P


def shortened(array):
    return jax.tree.map(lambda a: a.astype(jnp.bfloat16) if a.dtype == jnp.float32 else a, array)


def from_behind(value, axis, steps):
    count = lax.axis_size(axis)
    pairs = [(source, (source + steps) % count) for source in range(count)]
    return lax.ppermute(value, axis, pairs)


def expert_rows(x_rows, grad_rows, gate_weight, up_weight, down_weight):
    gate_pre = jnp.dot(x_rows, gate_weight, preferred_element_type=jnp.float32)
    up_pre = jnp.dot(x_rows, up_weight, preferred_element_type=jnp.float32)
    back_grad = lax.dot_general(
        grad_rows, down_weight, (((1,), (1,)), ((), ())), preferred_element_type=jnp.float32
    )
    logistic = jax.nn.sigmoid(gate_pre)
    swish = gate_pre * logistic
    score = jnp.sum(back_grad * swish * up_pre, axis=1).astype(jnp.bfloat16)
    d_gate = (back_grad * up_pre * logistic * (1.0 + gate_pre * (1.0 - logistic))).astype(
        jnp.bfloat16
    )
    d_up = (back_grad * swish).astype(jnp.bfloat16)
    pair_grad = lax.dot_general(
        d_gate, gate_weight, (((1,), (1,)), ((), ())), preferred_element_type=jnp.float32
    )
    pair_grad = pair_grad + lax.dot_general(
        d_up, up_weight, (((1,), (1,)), ((), ())), preferred_element_type=jnp.float32
    )
    return (pair_grad.astype(jnp.bfloat16), score)


def slot_table(ids_group, experts, capacity):
    groups, rows, picks = ids_group.shape
    flat_ids = ids_group.reshape(groups, rows * picks)
    onehot = (flat_ids[:, :, None] == jnp.arange(experts, dtype=jnp.int32)[None, None, :]).astype(
        jnp.int32
    )
    earlier = jnp.cumsum(onehot, axis=1) - onehot
    position = jnp.sum(earlier * onehot, axis=2)
    counts = jnp.sum(onehot, axis=1)
    group_index = jnp.arange(groups, dtype=jnp.int32)[:, None]
    target = flat_ids * (groups * capacity) + group_index * capacity + position
    return (target.reshape(-1), counts)


def expert_pass(x_group, grad_group, ids_group, seen, weights, send, bring_back, capacity):
    experts = seen.shape[0]
    groups, rows, width = x_group.shape
    picks = ids_group.shape[2]
    target, unused_counts = slot_table(ids_group, experts, capacity)
    total = experts * groups * capacity
    token_of = jnp.arange(groups * rows * picks, dtype=jnp.int32) // picks
    x_flat = x_group.reshape(groups * rows, width)
    grad_flat = grad_group.reshape(groups * rows, width)
    send_x = jnp.zeros((total, width), jnp.bfloat16).at[target].set(x_flat[token_of])
    send_grad = jnp.zeros((total, width), jnp.bfloat16).at[target].set(grad_flat[token_of])
    got_x, got_grad = send(
        (
            send_x.reshape(experts, groups * capacity, width),
            send_grad.reshape(experts, groups * capacity, width),
        )
    )
    slot = jnp.arange(groups * capacity, dtype=jnp.int32)
    limit = seen[:, slot // capacity]
    live = ((slot % capacity)[None, :] < limit).reshape(-1)
    block = min(256, total)
    padded = (total + block - 1) // block * block
    order = jnp.cumsum(live.astype(jnp.int32)) - 1
    used = jnp.sum(live.astype(jnp.int32))
    place = jnp.where(live, order, padded)
    pack_x = (
        jnp.zeros((padded, width), jnp.bfloat16)
        .at[place]
        .set(got_x.reshape(total, width), mode="drop")
    )
    pack_grad = (
        jnp.zeros((padded, width), jnp.bfloat16)
        .at[place]
        .set(got_grad.reshape(total, width), mode="drop")
    )
    gate_weight, up_weight, down_weight = weights

    def one_block(index, carry):
        block_grads, block_scores = carry
        start = index * block
        grad_rows, score_rows = expert_rows(
            lax.dynamic_slice_in_dim(pack_x, start, block, 0),
            lax.dynamic_slice_in_dim(pack_grad, start, block, 0),
            gate_weight,
            up_weight,
            down_weight,
        )
        return (
            lax.dynamic_update_slice_in_dim(block_grads, grad_rows, start, 0),
            lax.dynamic_update_slice_in_dim(block_scores, score_rows, start, 0),
        )

    empty = (jnp.zeros((padded, width), jnp.bfloat16), jnp.zeros((padded,), jnp.bfloat16))
    block_grads, block_scores = lax.fori_loop(0, (used + block - 1) // block, one_block, empty)
    source = jnp.minimum(place, padded - 1)
    out_rows = jnp.where(live[:, None], block_grads[source], jnp.zeros((), jnp.bfloat16))
    out_scores = jnp.where(live, block_scores[source], jnp.zeros((), jnp.bfloat16))
    ret_rows, ret_scores = bring_back(
        (
            out_rows.reshape(experts, groups * capacity, width),
            out_scores.reshape(experts, groups * capacity),
        )
    )
    pair_grad = ret_rows.reshape(total, width)[target].reshape(groups, rows, picks, width)
    pair_score = ret_scores.reshape(total)[target].reshape(groups, rows, picks)
    return (pair_grad, pair_score)


def on_device(inputs, grads_out, expert_ids, gate_values, w_gate, w_up, w_down):
    experts = lax.axis_size("expert")
    self_index = lax.axis_index("expert")
    x_all = inputs[0]
    grad_all = grads_out[0]
    ids_all = expert_ids[0]
    gates_all = gate_values[0]
    micro_count, rows, width = x_all.shape
    picks = ids_all.shape[2]
    capacity = min(rows, 8 * rows * picks // (3 * experts))
    unused_target, local_counts = slot_table(ids_all, experts, capacity)
    table = lax.all_gather(local_counts[None], "expert", axis=0, tiled=True)
    seen = jnp.take(table, self_index, axis=2)
    weights = (w_gate[0, 0], w_up[0, 0], w_down[0, 0])
    delivered = []
    scores = []

    def send_each(pair):
        return jax.tree.map(
            lambda part, own: part.astype(own.dtype),
            lax.all_to_all(shortened(pair), "expert", split_axis=0, concat_axis=0, tiled=True),
            pair,
        )

    def back_each(pair):
        return jax.tree.map(
            lambda part, own: part.astype(own.dtype),
            lax.all_to_all(shortened(pair), "expert", split_axis=0, concat_axis=0, tiled=True),
            pair,
        )

    for micro in range(micro_count):
        pair_grad, pair_score = expert_pass(
            x_all[micro : micro + 1],
            grad_all[micro : micro + 1],
            ids_all[micro : micro + 1],
            seen[:, micro : micro + 1],
            weights,
            send_each,
            back_each,
            capacity,
        )
        gates_part = gates_all[micro : micro + 1]
        combined = grad_all[micro : micro + 1].astype(jnp.float32) + jnp.sum(
            gates_part[..., None] * pair_grad.astype(jnp.float32), axis=2
        )
        moved = combined.astype(jnp.bfloat16)[None]
        score_part = pair_score.astype(jnp.float32)
        delivered.append(moved)
        scores.append(score_part)
    received = jnp.concatenate(delivered, axis=1)
    received = from_behind(received, "pipe", -1)
    gate_grad = jnp.concatenate(scores, axis=0)[None]
    return (received, gate_grad)


def solution(mesh):
    placed = (
        P("pipe", None, "expert", None),
        P("pipe", None, "expert", None),
        P("pipe", None, "expert", None),
        P("pipe", None, "expert", None),
        P("pipe", "expert", None, None),
        P("pipe", "expert", None, None),
        P("pipe", "expert", None, None),
    )
    return jax.shard_map(
        on_device,
        mesh=mesh,
        in_specs=placed,
        out_specs=(P("pipe", None, "expert", None), P("pipe", None, "expert", None)),
        check_vma=False,
    )
```

profile of v0, /device:TPU:0, one launch (start us, length us, event | category | flops | bytes accessed | tf_op | source)
XLA Modules:
  0.0 720.5 jit_solution(1070911775478979147)
XLA Ops:
  1.9 0.9 reduce-window.34
  3.3 1.1 slice_bitcast_fusion.3
  4.4 10.5 %scatter_custom_fusion = bf16[1024,2048]{1,0:T(8,128)(2,1)} fusion(s32[384]{0:T(512)S(1)} %fusion.59, bf16[]{:T(256)} %constant.139.clone.1, bf16[64,2048]{1,0:T(8,128)(2,1)S(1)} %get-tuple-element.165, s32[1024]{0:T(1024)S(1)} %pad_clamp_fusion.2), kind=kCustom, calls=%fused_computation.78 | custom fusion | bytes 4194306 | tf_op jit(solution)/shard_map/scatter | solution.py:63
  14.9 7.6 %all-to-all-start = ((bf16[32,32,2048]{2,1,0:T(8,128)(2,1)}), bf16[32,32,2048]{2,1,0:T(8,128)(2,1)}, u32[]{:S(2)}, u32[]{:S(2)}) async-start(bf16[32,32,2048]{2,1,0:T(8,128)(2,1)} %bitcast.143), calls=%async_computation | async-start | bytes 8388608 | tf_op jit(solution)/shard_map/all_to_all | solution.py:141
  22.6 10.5 %scatter_custom_fusion.2 = bf16[1024,2048]{1,0:T(8,128)(2,1)} fusion(s32[384]{0:T(512)S(1)} %fusion.59, bf16[]{:T(256)} %constant.139.clone.1, bf16[64,2048]{1,0:T(8,128)(2,1)S(1)} %get-tuple-element.163, s32[1024]{0:T(1024)S(1)} %pad_clamp_fusion.2), kind=kCustom, calls=%fused_computation.74 | custom fusion | bytes 4194306 | tf_op jit(solution)/shard_map/scatter | solution.py:62
  33.1 83.4 %all-to-all-done = bf16[32,32,2048]{2,1,0:T(8,128)(2,1)} async-done(((bf16[32,32,2048]{2,1,0:T(8,128)(2,1)}), bf16[32,32,2048]{2,1,0:T(8,128)(2,1)}, u32[]{:S(2)}, u32[]{:S(2)}) %all-to-all-start) | async-done | bytes 4194336 | tf_op jit(solution)/shard_map/all_to_all | solution.py:141
  116.5 4.3 all-to-all-start.1
  122.6 10.4 %scatter_custom_fusion.4 = bf16[1024,2048]{1,0:T(8,128)(2,1)} fusion(s32[384]{0:T(512)S(1)} %fusion.61, bf16[]{:T(256)} %constant.139.clone.1, bf16[64,2048]{1,0:T(8,128)(2,1)S(1)} %get-tuple-element.166, s32[1024]{0:T(1024)S(1)} %pad_clamp_fusion.2), kind=kCustom, calls=%fused_computation.70 | custom fusion | bytes 4194306 | tf_op jit(solution)/shard_map/scatter | solution.py:63
  133.1 81.6 %all-to-all-done.1 = bf16[32,32,2048]{2,1,0:T(8,128)(2,1)} async-done(((bf16[32,32,2048]{2,1,0:T(8,128)(2,1)}), bf16[32,32,2048]{2,1,0:T(8,128)(2,1)}, u32[]{:S(2)}, u32[]{:S(2)}) %all-to-all-start.1) | async-done | bytes 4194336 | tf_op jit(solution)/shard_map/all_to_all | solution.py:141
  214.6 4.0 all-to-all-start.3
  219.1 103.4 %all-gather.1 = s32[32,2,32]{2,1,0:T(2,128)S(1)} all-gather(s32[1,2,32]{2,1,0:T(2,128)S(1)} %bitcast.153), channel_id=2, replica_groups=mesh['pipe'=1,'expert'=32] {'expert'}, dimensions={0}, use_global_device_ids=true | all-gather | bytes 8448 | tf_op jit(solution)/shard_map/all_gather | solution.py:132
  326.3 10.6 %scatter_custom_fusion.6 = bf16[1024,2048]{1,0:T(8,128)(2,1)} fusion(s32[384]{0:T(512)S(1)} %fusion.61, bf16[]{:T(256)} %constant.139.clone.1, bf16[64,2048]{1,0:T(8,128)(2,1)S(1)} %get-tuple-element.164, s32[1024]{0:T(1024)S(1)} %pad_clamp_fusion.2), kind=kCustom, calls=%fused_computation.66 | custom fusion | bytes 4194306 | tf_op jit(solution)/shard_map/scatter | solution.py:62
  337.4 10.1 %scatter_custom_fusion.1 = bf16[1024,2048]{1,0:T(8,128)(2,1)} fusion(s32[1024]{0:T(1024)S(1)} %bitcast.156, bf16[1024,2048]{1,0:T(8,128)(2,1)} %bitcast.11, bf16[]{:T(256)} %constant.139.clone.1), kind=kCustom, calls=%fused_computation.76 | custom fusion | bytes 4194816 | tf_op jit(solution)/shard_map/scatter | solution.py:86
  347.4 10.1 %scatter_custom_fusion.3 = bf16[1024,2048]{1,0:T(8,128)(2,1)} fusion(s32[1024]{0:T(1024)S(1)} %bitcast.157, bf16[1024,2048]{1,0:T(8,128)(2,1)} %bitcast.15, bf16[]{:T(256)} %constant.139.clone.1), kind=kCustom, calls=%fused_computation.72 | custom fusion | bytes 4194816 | tf_op jit(solution)/shard_map/scatter | solution.py:81
  357.5 17.7 %all-to-all-start.4 = ((bf16[32,32,2048]{2,1,0:T(8,128)(2,1)}), bf16[32,32,2048]{2,1,0:T(8,128)(2,1)}, u32[]{:S(2)}, u32[]{:S(2)}) async-start(bf16[32,32,2048]{2,1,0:T(8,128)(2,1)} %bitcast.141), calls=%async_computation.4 | async-start | bytes 8388608 | tf_op jit(solution)/shard_map/all_to_all | solution.py:141
  375.3 2.5 broadcast.515.clone
  377.7 23.3 %while.25 = (s32[]{:T(128)}, bf16[1024,2048]{1,0:T(8,128)(2,1)}, bf16[1024]{0:T(1024)(128)(2,1)S(1)}, s32[]{:T(128)}, bf16[1024,2048]{1,0:T(8,128)(2,1)}, /*inde...) while((s32[]{:T(128)}, bf16[1024,2048]{1,0:T(8,128)(2,1)}, ...), condition=%wide.region_13.14_spmd, body=%wide.region_11.13_spmd.sunk | while | flops 4032102144 | bytes 69732112 | solution.py:106
  378.0 3.3 fusion.112
  381.3 2.3 fusion.113
  383.6 2.5 multiply_reduce_fusion.6
  386.1 1.1 fusion.114
  387.2 2.1 fusion.115
  389.5 3.3 fusion.112
  392.9 2.3 fusion.113
  395.2 2.5 multiply_reduce_fusion.6
  397.7 1.1 fusion.114
  398.8 2.0 fusion.115
  401.0 11.6 %gather_fusion = bf16[1024,2048]{1,0:T(8,128)(2,1)} fusion(bf16[1024,2048]{1,0:T(8,128)(2,1)} %get-tuple-element.100, s32[1024]{0:T(1024)S(1)} %broadcast_clamp_fusion.1), kind=kCustom, calls=%fused_computation.2 | custom fusion | bytes 8392704 | tf_op jit(solution)/shard_map/gather | solution.py:108
  412.6 10.1 %scatter_custom_fusion.5 = bf16[1024,2048]{1,0:T(8,128)(2,1)} fusion(s32[1024]{0:T(1024)S(1)} %bitcast.154, bf16[1024,2048]{1,0:T(8,128)(2,1)} %bitcast.31, bf16[]{:T(256)} %constant.139.clone.1), kind=kCustom, calls=%fused_computation.68 | custom fusion | bytes 4194816 | tf_op jit(solution)/shard_map/scatter | solution.py:86
  422.6 4.5 broadcast_select_fusion.1
  427.1 42.0 %all-to-all-done.4 = bf16[32,32,2048]{2,1,0:T(8,128)(2,1)} async-done(((bf16[32,32,2048]{2,1,0:T(8,128)(2,1)}), bf16[32,32,2048]{2,1,0:T(8,128)(2,1)}, u32[]{:S(2)}, u32[]{:S(2)}) %all-to-all-start.4) | async-done | bytes 4194336 | tf_op jit(solution)/shard_map/all_to_all | solution.py:141
  469.1 4.5 all-to-all-start.2
  473.6 10.0 %scatter_custom_fusion.7 = bf16[1024,2048]{1,0:T(8,128)(2,1)} fusion(s32[1024]{0:T(1024)S(1)} %bitcast.155, bf16[1024,2048]{1,0:T(8,128)(2,1)} %bitcast.34, bf16[]{:T(256)} %constant.139.clone.1), kind=kCustom, calls=%fused_computation.64 | custom fusion | bytes 4194816 | tf_op jit(solution)/shard_map/scatter | solution.py:81
  483.7 2.5 broadcast.515.clone.1
  486.2 23.1 %while.26 = (s32[]{:T(128)}, bf16[1024,2048]{1,0:T(8,128)(2,1)}, bf16[1024]{0:T(1024)(128)(2,1)S(1)}, s32[]{:T(128)}, bf16[1024,2048]{1,0:T(8,128)(2,1)}, /*inde...) while((s32[]{:T(128)}, bf16[1024,2048]{1,0:T(8,128)(2,1)}, ...), condition=%wide.region_27.28_spmd, body=%wide.region_25.27_spmd.sunk | while | flops 4032102144 | bytes 69732112 | solution.py:106
  486.2 3.3 fusion.124
  489.5 2.3 fusion.125
  491.8 2.5 multiply_reduce_fusion.7
  494.3 1.1 fusion.126
  495.5 2.1 fusion.127
  497.8 3.3 fusion.124
  501.1 2.3 fusion.125
  503.4 2.5 multiply_reduce_fusion.7
  505.9 1.1 fusion.126
  507.0 2.0 fusion.127
  509.2 11.5 %gather_fusion.2 = bf16[1024,2048]{1,0:T(8,128)(2,1)} fusion(bf16[1024,2048]{1,0:T(8,128)(2,1)} %get-tuple-element.101, s32[1024]{0:T(1024)S(1)} %broadcast_clamp_fusion), kind=kCustom, calls=%fused_computation.6 | custom fusion | bytes 8392704 | tf_op jit(solution)/shard_map/gather | solution.py:108
  520.8 4.5 broadcast_select_fusion
  525.3 42.2 %all-to-all-done.2 = bf16[32,32,2048]{2,1,0:T(8,128)(2,1)} async-done(((bf16[32,32,2048]{2,1,0:T(8,128)(2,1)}), bf16[32,32,2048]{2,1,0:T(8,128)(2,1)}, u32[]{:S(2)}, u32[]{:S(2)}) %all-to-all-start.2) | async-done | bytes 4194336 | tf_op jit(solution)/shard_map/all_to_all | solution.py:148
  567.6 4.0 all-to-all-start.5
  571.9 7.1 gather_fusion.1
  579.0 2.2 reshape.911
  581.2 84.3 %all-to-all-done.5 = bf16[32,32,2048]{2,1,0:T(8,128)(2,1)} async-done(((bf16[32,32,2048]{2,1,0:T(8,128)(2,1)}), bf16[32,32,2048]{2,1,0:T(8,128)(2,1)}, u32[]{:S(2)}, u32[]{:S(2)}) %all-to-all-start.5) | async-done | bytes 4194336 | tf_op jit(solution)/shard_map/all_to_all | solution.py:148
  665.5 7.1 gather_fusion.3
  672.6 2.1 reshape.912
  674.7 3.9 multiply_reduce_fusion.3
  678.7 1.5 multiply_reduce_fusion.2
  680.4 6.8 gather_fusion.4
  687.3 6.8 gather_fusion.6
  694.9 4.0 all-to-all-start.7
  699.5 6.5 all-to-all-done.7
  706.0 2.6 all-to-all-start.6
  708.7 2.8 gather_fusion.7
  711.8 3.9 all-to-all-done.6
  715.9 2.8 gather_fusion.5
  (147 shorter events, 11.7 us)
Async XLA Ops:
  4.4 18.2 %copy-start.10 = (s32[384]{0:T(512)}, s32[384]{0:T(512)S(1)}, u32[]{:S(2)}) copy-start(s32[384]{0:T(512)S(1)} %fusion.59) | copy-start | bytes 4612
  14.9 7.6 %copy-start.2 = (bf16[1,2,64,2048]{3,2,1,0:T(8,128)(2,1)S(1)}, bf16[1,2,64,2048]{3,2,1,0:T(8,128)(2,1)}, u32[]{:S(2)}) copy-start(bf16[1,2,64,2048]{3,2,1,0:T(8,128)(2,1)} %param.11) | copy-start | bytes 1572868
  14.9 101.5 %all-to-all-start = ((bf16[32,32,2048]{2,1,0:T(8,128)(2,1)}), bf16[32,32,2048]{2,1,0:T(8,128)(2,1)}, u32[]{:S(2)}, u32[]{:S(2)}) async-start(bf16[32,32,2048]{2,1,0:T(8,128)(2,1)} %bitcast.143), calls=%async_computation | async-start | bytes 8388608 | tf_op jit(solution)/shard_map/all_to_all | solution.py:141
  116.5 98.2 %all-to-all-start.1 = ((bf16[32,32,2048]{2,1,0:T(8,128)(2,1)}), bf16[32,32,2048]{2,1,0:T(8,128)(2,1)}, u32[]{:S(2)}, u32[]{:S(2)}) async-start(bf16[32,32,2048]{2,1,0:T(8,128)(2,1)} %bitcast.142), calls=%async_computation.1 | async-start | bytes 8388608 | tf_op jit(solution)/shard_map/all_to_all | solution.py:141
  214.6 4.1 copy-start.3
  214.6 142.9 %all-to-all-start.3 = ((bf16[32,32,2048]{2,1,0:T(8,128)(2,1)}), bf16[32,32,2048]{2,1,0:T(8,128)(2,1)}, u32[]{:S(2)}, u32[]{:S(2)}) async-start(bf16[32,32,2048]{2,1,0:T(8,128)(2,1)} %bitcast.140), calls=%async_computation.3 | async-start | bytes 8388608 | tf_op jit(solution)/shard_map/all_to_all | solution.py:141
  322.7 2.5 copy-start.8
  322.7 2.2 copy-start.6
  322.8 2.5 copy-start.4
  357.5 111.6 %all-to-all-start.4 = ((bf16[32,32,2048]{2,1,0:T(8,128)(2,1)}), bf16[32,32,2048]{2,1,0:T(8,128)(2,1)}, u32[]{:S(2)}, u32[]{:S(2)}) async-start(bf16[32,32,2048]{2,1,0:T(8,128)(2,1)} %bitcast.141), calls=%async_computation.4 | async-start | bytes 8388608 | tf_op jit(solution)/shard_map/all_to_all | solution.py:141
  377.9 3.4 copy-start.13
  378.0 5.6 copy-start.15
  383.6 2.5 copy-start.17
  389.5 3.3 copy-start.13
  389.5 5.6 copy-start.15
  395.2 2.5 copy-start.17
  469.1 98.4 %all-to-all-start.2 = ((bf16[32,32,2048]{2,1,0:T(8,128)(2,1)}), bf16[32,32,2048]{2,1,0:T(8,128)(2,1)}, u32[]{:S(2)}, u32[]{:S(2)}) async-start(bf16[32,32,2048]{2,1,0:T(8,128)(2,1)} %broadcast_select_fusion.1), calls=%async_computation.2 | async-start | bytes 8388608 | tf_op jit(solution)/shard_map/all_to_all | solution.py:148
  486.2 3.3 copy-start.14
  486.2 5.6 copy-start.16
  491.8 2.5 copy-start.18
  497.7 3.3 copy-start.14
  497.8 5.6 copy-start.16
  503.4 2.5 copy-start.18
  525.3 46.3 %copy-start.12 = (f32[1,2,64,6]{2,1,3,0:T(2,128)S(1)}, f32[1,2,64,6]{2,1,3,0:T(2,128)}, u32[]{:S(2)}) copy-start(f32[1,2,64,6]{2,1,3,0:T(2,128)} %param.14) | copy-start | bytes 9220
  525.3 46.5 %copy-start.11 = (s32[384]{0:T(512)S(1)}, s32[384]{0:T(512)}, u32[]{:S(2)}) copy-start(s32[384]{0:T(512)} %copy-done.10) | copy-start | bytes 4612
  567.6 97.9 %all-to-all-start.5 = ((bf16[32,32,2048]{2,1,0:T(8,128)(2,1)}), bf16[32,32,2048]{2,1,0:T(8,128)(2,1)}, u32[]{:S(2)}, u32[]{:S(2)}) async-start(bf16[32,32,2048]{2,1,0:T(8,128)(2,1)} %broadcast_select_fusion), calls=%async_computation.5 | async-start | bytes 8388608 | tf_op jit(solution)/shard_map/all_to_all | solution.py:148
  674.7 3.9 copy-start
  674.7 5.4 copy-start.1
  680.2 14.0 %copy-start.5 = (s32[32]{0:T(128)S(1)}, s32[32]{0:T(128)}, u32[]{:S(2)}) copy-start(s32[32]{0:T(128)} %copy-done.4) | copy-start | bytes 388
  680.2 14.0 %copy-start.7 = (s32[32]{0:T(128)S(1)}, s32[32]{0:T(128)}, u32[]{:S(2)}) copy-start(s32[32]{0:T(128)} %copy-done.6) | copy-start | bytes 388
  680.2 14.0 %copy-start.9 = (s32[32]{0:T(128)S(1)}, s32[32]{0:T(128)}, u32[]{:S(2)}) copy-start(s32[32]{0:T(128)} %copy-done.8) | copy-start | bytes 388
  680.4 39.1 %collective-permute-start = (bf16[1,2,64,2048]{3,2,1,0:T(8,128)(2,1)S(1)}, bf16[1,2,64,2048]{3,2,1,0:T(8,128)(2,1)S(1)}, u32[]{:S(2)}, u32[]{:S(2)}) collective-permute-start(bf16[1,2,64,2048]{3,2,1,0:T(8,128)(2,1)S(1)} %pad_maximum_fusion), channel_id=1, source_target_pairs={{0,0},{1,1},{2,2},{3,3},{4,4},{5,5},{6,6},{7,7},{8,8},{9,9},{10,10... | collective-permute-start | bytes 1572872 | tf_op jit(solution)/shard_map/ppermute | solution.py:14
  694.9 11.0 %all-to-all-start.7 = ((bf16[32,1,32]{2,1,0:T(2,128)(2,1)}), bf16[32,1,32]{2,1,0:T(2,128)(2,1)S(1)}, u32[]{:S(2)}, u32[]{:S(2)}) async-start(bf16[32,1,32]{2,1,0:T(2,128)(2,1)} %copy.105), calls=%async_computation.7 | async-start | bytes 32768 | tf_op jit(solution)/shard_map/all_to_all | solution.py:148
  706.0 9.7 %all-to-all-start.6 = ((bf16[32,1,32]{2,1,0:T(2,128)(2,1)}), bf16[32,1,32]{2,1,0:T(2,128)(2,1)S(1)}, u32[]{:S(2)}, u32[]{:S(2)}) async-start(bf16[32,1,32]{2,1,0:T(2,128)(2,1)} %copy.104), calls=%async_computation.6 | async-start | bytes 32768 | tf_op jit(solution)/shard_map/all_to_all | solution.py:148
where the time goes:
time: 729 us; the launch traced here: 721 us
  waiting for transfers between devices  344 us (47%)
  local copies, waits for them, and re-layouts  157 us (22%)
  blocking collectives  103 us (14%)
  starting transfers between devices  48.7 us (7%)
  matrix products  45.1 us (6%)
  other arithmetic  19.2 us (3%)
    all_to_all x4, waiting for transfers between devices, send_each(): lax.all_to_all(shortened(pair), 'expert', split_axis=0, concat_axis=0, ti...  207 us
    all_to_all x4, waiting for transfers between devices, back_each(): lax.all_to_all(shortened(pair), 'expert', split_axis=0, concat_axis=0, ti...  137 us
    all_gather x1, blocking collectives, on_device(): table = lax.all_gather(local_counts[None], 'expert', axis=0, tiled=True)  103 us
    all_to_all x4, starting transfers between devices, send_each(): lax.all_to_all(shortened(pair), 'expert', split_axis=0, concat_axis=0, ti...  33.6 us
    gather x2, local copies, waits for them, and re-layouts, expert_pass(): block_grads[source]  23.1 us
    scatter x2, local copies, waits for them, and re-layouts, expert_pass(): jnp.zeros((total, width), jnp.bfloat16).at[target].set(x_flat[token_of])  21.1 us
    scatter x2, local copies, waits for them, and re-layouts, expert_pass(): jnp.zeros((total, width), jnp.bfloat16).at[target].set(grad_flat[token_of])  20.9 us
    scatter x2, local copies, waits for them, and re-layouts, expert_pass(): pack_grad = jnp.zeros((padded, width), jnp.bfloat16).at[place].set(got_gr...  20.1 us
  transfers between devices with their start and end apart: 9, of which 7 were waited for; matrix products, arithmetic and copies ran while one was open for 27% of the time, Pallas kernels for 0%

commit v1 on v0

--- a/solution.py
+++ b/solution.py
@@ -2,6 +2,18 @@
 import jax.numpy as jnp
 from jax import lax
 from jax.sharding import PartitionSpec as P
+
+
+def doubled_up(x, axis, dim):
+    ways, here, lap = (lax.axis_size(axis), lax.axis_index(axis), x.shape[dim])
+    line, have = (x, 1)
+    while have < ways:
+        line = jnp.concatenate(
+            [line, lax.ppermute(line, axis, [(d, (d - have) % ways) for d in range(ways)])],
+            axis=dim,
+        )
+        have = 2 * have
+    return jnp.roll(line, here * lap, axis=dim)
 
 
 def shortened(array):
@@ -129,7 +141,7 @@
     picks = ids_all.shape[2]
     capacity = min(rows, 8 * rows * picks // (3 * experts))
     unused_target, local_counts = slot_table(ids_all, experts, capacity)
-    table = lax.all_gather(local_counts[None], "expert", axis=0, tiled=True)
+    table = doubled_up(local_counts[None], "expert", 0)
     seen = jnp.take(table, self_index, axis=2)
     weights = (w_gate[0, 0], w_up[0, 0], w_down[0, 0])
     delivered = []

time: 729 us -> 698 us (0.957)
  blocking collectives: 103 us -> 0 us
  waiting for transfers between devices: 344 us -> 418 us
    all_gather x1 -> x0, blocking collectives: 103 us -> none  [on_device(): table = lax.all_gather(local_counts[None], 'expert', axis=0, tiled=True)]
    all_to_all x4, waiting for transfers between devices: 207 us -> 267 us  [send_each(): lax.all_to_all(shortened(pair), 'expert', split_axis=0, concat_axis=0, ti...]
    ppermute x0 -> x5, waiting for transfers between devices: none -> 13.7 us  [doubled_up(): lax.ppermute(line, axis, [(d, (d - have) % ways) for d in range(ways)])]
    all_to_all x4, starting transfers between devices: 33.6 us -> 22.1 us  [send_each(): lax.all_to_all(shortened(pair), 'expert', split_axis=0, concat_axis=0, ti...]
    ppermute x0 -> x5, starting transfers between devices: none -> 8.09 us  [doubled_up(): lax.ppermute(line, axis, [(d, (d - have) % ways) for d in range(ways)])]
  transfers between devices with their start and end apart: 9 -> 14, of which waited for: 7 -> 12; matrix products, arithmetic and copies ran while one was open for 27% -> 28% of each run, Pallas kernels for 0% -> 0%
where the time goes in v1:
time: 698 us; the launch traced here: 689 us
  waiting for transfers between devices  418 us (60%)
  local copies, waits for them, and re-layouts  158 us (23%)
  starting transfers between devices  45.3 us (6%)
  matrix products  45.1 us (6%)
  other arithmetic  19.2 us (3%)
    all_to_all x4, waiting for transfers between devices, send_each(): lax.all_to_all(shortened(pair), 'expert', split_axis=0, concat_axis=0, ti...  267 us
    all_to_all x4, waiting for transfers between devices, back_each(): lax.all_to_all(shortened(pair), 'expert', split_axis=0, concat_axis=0, ti...  137 us
    gather x2, local copies, waits for them, and re-layouts, expert_pass(): block_grads[source]  23.1 us
    all_to_all x4, starting transfers between devices, send_each(): lax.all_to_all(shortened(pair), 'expert', split_axis=0, concat_axis=0, ti...  22.1 us
    scatter x2, local copies, waits for them, and re-layouts, expert_pass(): jnp.zeros((total, width), jnp.bfloat16).at[target].set(x_flat[token_of])  21.1 us
    scatter x2, local copies, waits for them, and re-layouts, expert_pass(): jnp.zeros((total, width), jnp.bfloat16).at[target].set(grad_flat[token_of])  21 us
    scatter x2, local copies, waits for them, and re-layouts, expert_pass(): pack_grad = jnp.zeros((padded, width), jnp.bfloat16).at[place].set(got_gr...  20.1 us
    scatter x2, local copies, waits for them, and re-layouts, expert_pass(): pack_x = jnp.zeros((padded, width), jnp.bfloat16).at[place].set(got_x.res...  20.1 us
  transfers between devices with their start and end apart: 14, of which 12 were waited for; matrix products, arithmetic and copies ran while one was open for 28% of the time, Pallas kernels for 0%

profile of v1, /device:TPU:0, one launch (start us, length us, event | category | flops | bytes accessed | tf_op | source)
XLA Modules:
  0.0 688.6 jit_solution(8295650873138935281)
XLA Ops:
  1.7 6.4 collective-permute-start
  12.5 3.0 collective-permute-done.1
  16.1 3.1 collective-permute-done.2
  19.6 3.2 collective-permute-done.3
  23.1 4.5 collective-permute-done.4
  28.9 10.5 %scatter_custom_fusion = bf16[1024,2048]{1,0:T(8,128)(2,1)} fusion(s32[384]{0:T(512)S(1)} %fusion.59, bf16[]{:T(256)} %constant.155.clone.1, bf16[64,2048]{1,0:T(8,128)(2,1)S(1)} %get-tuple-element.165, s32[1024]{0:T(1024)S(1)} %get-tuple-element.195), kind=kCustom, calls=%fused_computation.78 | custom fusion | bytes 4194306 | tf_op jit(solution)/shard_map/scatter | solution.py:75
  39.4 9.3 %all-to-all-start = ((bf16[32,32,2048]{2,1,0:T(8,128)(2,1)}), bf16[32,32,2048]{2,1,0:T(8,128)(2,1)}, u32[]{:S(2)}, u32[]{:S(2)}) async-start(bf16[32,32,2048]{2,1,0:T(8,128)(2,1)} %bitcast.146), calls=%async_computation | async-start | bytes 8388608 | tf_op jit(solution)/shard_map/all_to_all | solution.py:153
  48.8 10.5 %scatter_custom_fusion.2 = bf16[1024,2048]{1,0:T(8,128)(2,1)} fusion(s32[384]{0:T(512)S(1)} %fusion.59, bf16[]{:T(256)} %constant.155.clone.1, bf16[64,2048]{1,0:T(8,128)(2,1)S(1)} %get-tuple-element.163, s32[1024]{0:T(1024)S(1)} %get-tuple-element.195), kind=kCustom, calls=%fused_computation.74 | custom fusion | bytes 4194306 | tf_op jit(solution)/shard_map/scatter | solution.py:74
  59.3 83.4 %all-to-all-done = bf16[32,32,2048]{2,1,0:T(8,128)(2,1)} async-done(((bf16[32,32,2048]{2,1,0:T(8,128)(2,1)}), bf16[32,32,2048]{2,1,0:T(8,128)(2,1)}, u32[]{:S(2)}, u32[]{:S(2)}) %all-to-all-start) | async-done | bytes 4194336 | tf_op jit(solution)/shard_map/all_to_all | solution.py:153
  142.7 4.3 all-to-all-start.1
  148.8 10.5 %scatter_custom_fusion.4 = bf16[1024,2048]{1,0:T(8,128)(2,1)} fusion(s32[384]{0:T(512)S(1)} %fusion.61, bf16[]{:T(256)} %constant.155.clone.1, bf16[64,2048]{1,0:T(8,128)(2,1)S(1)} %get-tuple-element.166, s32[1024]{0:T(1024)S(1)} %get-tuple-element.195), kind=kCustom, calls=%fused_computation.70 | custom fusion | bytes 4194306 | tf_op jit(solution)/shard_map/scatter | solution.py:75
  159.3 81.5 %all-to-all-done.1 = bf16[32,32,2048]{2,1,0:T(8,128)(2,1)} async-done(((bf16[32,32,2048]{2,1,0:T(8,128)(2,1)}), bf16[32,32,2048]{2,1,0:T(8,128)(2,1)}, u32[]{:S(2)}, u32[]{:S(2)}) %all-to-all-start.1) | async-done | bytes 4194336 | tf_op jit(solution)/shard_map/all_to_all | solution.py:153
  240.9 4.5 all-to-all-start.3
  247.9 10.6 %scatter_custom_fusion.6 = bf16[1024,2048]{1,0:T(8,128)(2,1)} fusion(s32[384]{0:T(512)S(1)} %fusion.61, bf16[]{:T(256)} %constant.155.clone.1, bf16[64,2048]{1,0:T(8,128)(2,1)S(1)} %get-tuple-element.164, s32[1024]{0:T(1024)S(1)} %get-tuple-element.195), kind=kCustom, calls=%fused_computation.66 | custom fusion | bytes 4194306 | tf_op jit(solution)/shard_map/scatter | solution.py:74
  258.8 10.1 %scatter_custom_fusion.1 = bf16[1024,2048]{1,0:T(8,128)(2,1)} fusion(s32[1024]{0:T(1024)S(1)} %bitcast.162, bf16[1024,2048]{1,0:T(8,128)(2,1)} %bitcast.11, bf16[]{:T(256)} %constant.155.clone.1), kind=kCustom, calls=%fused_computation.76 | custom fusion | bytes 4194816 | tf_op jit(solution)/shard_map/scatter | solution.py:98
  268.8 10.0 %scatter_custom_fusion.3 = bf16[1024,2048]{1,0:T(8,128)(2,1)} fusion(s32[1024]{0:T(1024)S(1)} %bitcast.163, bf16[1024,2048]{1,0:T(8,128)(2,1)} %bitcast.15, bf16[]{:T(256)} %constant.155.clone.1), kind=kCustom, calls=%fused_computation.72 | custom fusion | bytes 4194816 | tf_op jit(solution)/shard_map/scatter | solution.py:93
  278.9 60.4 %all-to-all-done.3 = bf16[32,32,2048]{2,1,0:T(8,128)(2,1)} async-done(((bf16[32,32,2048]{2,1,0:T(8,128)(2,1)}), bf16[32,32,2048]{2,1,0:T(8,128)(2,1)}, u32[]{:S(2)}, u32[]{:S(2)}) %all-to-all-start.3) | async-done | bytes 4194336 | tf_op jit(solution)/shard_map/all_to_all | solution.py:153
  339.2 4.0 all-to-all-start.4
  343.3 2.5 broadcast.516.clone
  345.8 23.2 %while.25 = (s32[]{:T(128)}, bf16[1024,2048]{1,0:T(8,128)(2,1)}, bf16[1024]{0:T(1024)(128)(2,1)S(1)}, s32[]{:T(128)}, bf16[1024,2048]{1,0:T(8,128)(2,1)}, /*inde...) while((s32[]{:T(128)}, bf16[1024,2048]{1,0:T(8,128)(2,1)}, ...), condition=%wide.region_13.14_spmd, body=%wide.region_11.13_spmd.sunk | while | flops 4032102144 | bytes 69732112 | solution.py:118
  346.0 3.3 fusion.112
  349.4 2.3 fusion.113
  351.6 2.5 multiply_reduce_fusion.6
  355.3 2.0 fusion.115
  357.5 3.3 fusion.112
  360.8 2.3 fusion.113
  363.1 2.5 multiply_reduce_fusion.6
  366.8 2.1 fusion.115
  369.0 11.6 %gather_fusion = bf16[1024,2048]{1,0:T(8,128)(2,1)} fusion(bf16[1024,2048]{1,0:T(8,128)(2,1)} %get-tuple-element.100, s32[1024]{0:T(1024)S(1)} %broadcast_clamp_fusion.1), kind=kCustom, calls=%fused_computation.2 | custom fusion | bytes 8392704 | tf_op jit(solution)/shard_map/gather | solution.py:120
  380.6 10.1 %scatter_custom_fusion.5 = bf16[1024,2048]{1,0:T(8,128)(2,1)} fusion(s32[1024]{0:T(1024)S(1)} %bitcast.160, bf16[1024,2048]{1,0:T(8,128)(2,1)} %bitcast.31, bf16[]{:T(256)} %constant.155.clone.1), kind=kCustom, calls=%fused_computation.68 | custom fusion | bytes 4194816 | tf_op jit(solution)/shard_map/scatter | solution.py:98
  390.6 4.5 broadcast_select_fusion.1
  395.1 42.1 %all-to-all-done.4 = bf16[32,32,2048]{2,1,0:T(8,128)(2,1)} async-done(((bf16[32,32,2048]{2,1,0:T(8,128)(2,1)}), bf16[32,32,2048]{2,1,0:T(8,128)(2,1)}, u32[]{:S(2)}, u32[]{:S(2)}) %all-to-all-start.4) | async-done | bytes 4194336 | tf_op jit(solution)/shard_map/all_to_all | solution.py:153
  437.2 4.5 all-to-all-start.2
  441.7 10.0 %scatter_custom_fusion.7 = bf16[1024,2048]{1,0:T(8,128)(2,1)} fusion(s32[1024]{0:T(1024)S(1)} %bitcast.161, bf16[1024,2048]{1,0:T(8,128)(2,1)} %bitcast.34, bf16[]{:T(256)} %constant.155.clone.1), kind=kCustom, calls=%fused_computation.64 | custom fusion | bytes 4194816 | tf_op jit(solution)/shard_map/scatter | solution.py:93
  451.7 2.5 broadcast.516.clone.1
  454.2 23.1 %while.26 = (s32[]{:T(128)}, bf16[1024,2048]{1,0:T(8,128)(2,1)}, bf16[1024]{0:T(1024)(128)(2,1)S(1)}, s32[]{:T(128)}, bf16[1024,2048]{1,0:T(8,128)(2,1)}, /*inde...) while((s32[]{:T(128)}, bf16[1024,2048]{1,0:T(8,128)(2,1)}, ...), condition=%wide.region_27.28_spmd, body=%wide.region_25.27_spmd.sunk | while | flops 4032102144 | bytes 69732112 | solution.py:118
  454.2 3.3 fusion.124
  457.6 2.3 fusion.125
  459.8 2.5 multiply_reduce_fusion.7
  462.4 1.1 fusion.126
  463.5 2.1 fusion.127
  465.8 3.3 fusion.124
  469.2 2.3 fusion.125
  471.4 2.5 multiply_reduce_fusion.7
  475.1 2.0 fusion.127
  477.3 11.6 %gather_fusion.2 = bf16[1024,2048]{1,0:T(8,128)(2,1)} fusion(bf16[1024,2048]{1,0:T(8,128)(2,1)} %get-tuple-element.101, s32[1024]{0:T(1024)S(1)} %get-tuple-element.196), kind=kCustom, calls=%fused_computation.6 | custom fusion | bytes 8392704 | tf_op jit(solution)/shard_map/gather | solution.py:120
  488.9 4.5 broadcast_select_fusion
  493.4 42.2 %all-to-all-done.2 = bf16[32,32,2048]{2,1,0:T(8,128)(2,1)} async-done(((bf16[32,32,2048]{2,1,0:T(8,128)(2,1)}), bf16[32,32,2048]{2,1,0:T(8,128)(2,1)}, u32[]{:S(2)}, u32[]{:S(2)}) %all-to-all-start.2) | async-done | bytes 4194336 | tf_op jit(solution)/shard_map/all_to_all | solution.py:160
  535.6 4.0 all-to-all-start.5
  539.9 7.1 %gather_fusion.1 = bf16[384,2048]{1,0:T(8,128)(2,1)S(1)} fusion(bf16[1024,2048]{1,0:T(8,128)(2,1)} %bitcast.20, s32[1024]{0:T(1024)S(1)} %pad_clamp_fusion.1), kind=kCustom, calls=%fused_computation.3 | custom fusion | bytes 3147264 | tf_op jit(solution)/shard_map/gather | solution.py:128
  547.0 2.2 reshape.911
  549.2 84.3 %all-to-all-done.5 = bf16[32,32,2048]{2,1,0:T(8,128)(2,1)} async-done(((bf16[32,32,2048]{2,1,0:T(8,128)(2,1)}), bf16[32,32,2048]{2,1,0:T(8,128)(2,1)}, u32[]{:S(2)}, u32[]{:S(2)}) %all-to-all-start.5) | async-done | bytes 4194336 | tf_op jit(solution)/shard_map/all_to_all | solution.py:160
  633.5 7.1 %gather_fusion.3 = bf16[384,2048]{1,0:T(8,128)(2,1)S(1)} fusion(bf16[1024,2048]{1,0:T(8,128)(2,1)} %bitcast.37, s32[1024]{0:T(1024)S(1)} %pad_clamp_fusion), kind=kCustom, calls=%fused_computation.7 | custom fusion | bytes 3147264 | tf_op jit(solution)/shard_map/gather | solution.py:128
  640.6 2.1 reshape.912
  642.8 3.9 multiply_reduce_fusion.3
  646.7 1.5 multiply_reduce_fusion.2
  648.5 6.8 gather_fusion.4
  655.4 6.8 gather_fusion.6
  663.0 4.0 all-to-all-start.7
  667.6 6.5 all-to-all-done.7
  674.0 2.6 all-to-all-start.6
  676.7 2.8 gather_fusion.7
  679.8 3.9 all-to-all-done.6
  683.9 2.8 gather_fusion.5
  (172 shorter events, 19.5 us)
Async XLA Ops:
  1.7 10.2 %collective-permute-start = (s32[1,2,32]{2,1,0:T(2,128)S(1)}, s32[1,2,32]{2,1,0:T(2,128)S(1)}, u32[]{:S(2)}, u32[]{:S(2)}) collective-permute-start(s32[1,2,32]{2,1,0:T(2,128)S(1)} %bitcast.151), channel_id=1, source_target_pairs={{0,31},{1,0},{2,1},{3,2},{4,3},{5,4},{6,5},{7,6},{8,7},{9,8},{10,9... | collective-permute-start | bytes 776 | tf_op jit(solution)/shard_map/ppermute | solution.py:12
  11.9 36.9 %copy-start.11 = (s32[384]{0:T(512)}, s32[384]{0:T(512)S(1)}, u32[]{:S(2)}) copy-start(s32[384]{0:T(512)S(1)} %fusion.59) | copy-start | bytes 4612
  11.9 3.6 collective-permute-start.1
  15.5 3.6 collective-permute-start.2
  19.2 3.7 collective-permute-start.3
  22.8 4.7 collective-permute-start.4
  22.9 222.4 %copy-start.9 = (s32[32]{0:T(128)}, s32[32]{0:T(128)S(1)}, u32[]{:S(2)}) copy-start(s32[32]{0:T(128)S(1)} %and_select_fusion.1) | copy-start | bytes 388
  27.8 217.5 %copy-start.5 = (s32[32]{0:T(128)}, s32[32]{0:T(128)S(1)}, u32[]{:S(2)}) copy-start(s32[32]{0:T(128)S(1)} %get-tuple-element.181) | copy-start | bytes 388
  27.8 217.5 %copy-start.7 = (s32[32]{0:T(128)}, s32[32]{0:T(128)S(1)}, u32[]{:S(2)}) copy-start(s32[32]{0:T(128)S(1)} %get-tuple-element.182) | copy-start | bytes 388
  27.9 11.5 %copy-start.3 = (pred[32,32]{1,0:T(8,128)(4,1)}, pred[32,32]{1,0:T(8,128)(4,1)S(1)}, u32[]{:S(2)}) copy-start(pred[32,32]{1,0:T(8,128)(4,1)S(1)} %get-tuple-element.192) | copy-start | bytes 3076
  39.4 9.4 %copy-start.2 = (bf16[1,2,64,2048]{3,2,1,0:T(8,128)(2,1)S(1)}, bf16[1,2,64,2048]{3,2,1,0:T(8,128)(2,1)}, u32[]{:S(2)}) copy-start(bf16[1,2,64,2048]{3,2,1,0:T(8,128)(2,1)} %param.11) | copy-start | bytes 1572868
  39.4 103.3 %all-to-all-start = ((bf16[32,32,2048]{2,1,0:T(8,128)(2,1)}), bf16[32,32,2048]{2,1,0:T(8,128)(2,1)}, u32[]{:S(2)}, u32[]{:S(2)}) async-start(bf16[32,32,2048]{2,1,0:T(8,128)(2,1)} %bitcast.146), calls=%async_computation | async-start | bytes 8388608 | tf_op jit(solution)/shard_map/all_to_all | solution.py:153
  142.7 98.2 %all-to-all-start.1 = ((bf16[32,32,2048]{2,1,0:T(8,128)(2,1)}), bf16[32,32,2048]{2,1,0:T(8,128)(2,1)}, u32[]{:S(2)}, u32[]{:S(2)}) async-start(bf16[32,32,2048]{2,1,0:T(8,128)(2,1)} %bitcast.145), calls=%async_computation.1 | async-start | bytes 8388608 | tf_op jit(solution)/shard_map/all_to_all | solution.py:153
  240.9 98.4 %all-to-all-start.3 = ((bf16[32,32,2048]{2,1,0:T(8,128)(2,1)}), bf16[32,32,2048]{2,1,0:T(8,128)(2,1)}, u32[]{:S(2)}, u32[]{:S(2)}) async-start(bf16[32,32,2048]{2,1,0:T(8,128)(2,1)} %bitcast.143), calls=%async_computation.3 | async-start | bytes 8388608 | tf_op jit(solution)/shard_map/all_to_all | solution.py:153
  339.2 97.9 %all-to-all-start.4 = ((bf16[32,32,2048]{2,1,0:T(8,128)(2,1)}), bf16[32,32,2048]{2,1,0:T(8,128)(2,1)}, u32[]{:S(2)}, u32[]{:S(2)}) async-start(bf16[32,32,2048]{2,1,0:T(8,128)(2,1)} %bitcast.144), calls=%async_computation.4 | async-start | bytes 8388608 | tf_op jit(solution)/shard_map/all_to_all | solution.py:153
  346.0 3.4 copy-start.14
  346.0 5.6 copy-start.16
  351.6 2.5 copy-start.18
  357.5 3.3 copy-start.14
  357.5 5.6 copy-start.16
  363.1 2.5 copy-start.18
  437.2 98.4 %all-to-all-start.2 = ((bf16[32,32,2048]{2,1,0:T(8,128)(2,1)}), bf16[32,32,2048]{2,1,0:T(8,128)(2,1)}, u32[]{:S(2)}, u32[]{:S(2)}) async-start(bf16[32,32,2048]{2,1,0:T(8,128)(2,1)} %broadcast_select_fusion.1), calls=%async_computation.2 | async-start | bytes 8388608 | tf_op jit(solution)/shard_map/all_to_all | solution.py:160
  454.2 3.3 copy-start.15
  454.2 5.6 copy-start.17
  459.8 2.5 copy-start.19
  465.8 3.3 copy-start.15
  465.8 5.6 copy-start.17
  471.4 2.5 copy-start.19
  477.3 11.6 %copy-start.4 = (pred[32,32]{1,0:T(8,128)(4,1)S(1)}, pred[32,32]{1,0:T(8,128)(4,1)}, u32[]{:S(2)}) copy-start(pred[32,32]{1,0:T(8,128)(4,1)} %copy-done.3) | copy-start | bytes 3076
  493.4 46.2 %copy-start.13 = (f32[1,2,64,6]{2,1,3,0:T(2,128)S(1)}, f32[1,2,64,6]{2,1,3,0:T(2,128)}, u32[]{:S(2)}) copy-start(f32[1,2,64,6]{2,1,3,0:T(2,128)} %param.14) | copy-start | bytes 9220
  493.4 46.5 %copy-start.12 = (s32[384]{0:T(512)S(1)}, s32[384]{0:T(512)}, u32[]{:S(2)}) copy-start(s32[384]{0:T(512)} %copy-done.11) | copy-start | bytes 4612
  535.6 97.9 %all-to-all-start.5 = ((bf16[32,32,2048]{2,1,0:T(8,128)(2,1)}), bf16[32,32,2048]{2,1,0:T(8,128)(2,1)}, u32[]{:S(2)}, u32[]{:S(2)}) async-start(bf16[32,32,2048]{2,1,0:T(8,128)(2,1)} %broadcast_select_fusion), calls=%async_computation.5 | async-start | bytes 8388608 | tf_op jit(solution)/shard_map/all_to_all | solution.py:160
  642.8 3.9 copy-start
  642.8 5.4 copy-start.1
  648.2 14.0 %copy-start.6 = (s32[32]{0:T(128)S(1)}, s32[32]{0:T(128)}, u32[]{:S(2)}) copy-start(s32[32]{0:T(128)} %copy-done.5) | copy-start | bytes 388
  648.2 14.0 %copy-start.8 = (s32[32]{0:T(128)S(1)}, s32[32]{0:T(128)}, u32[]{:S(2)}) copy-start(s32[32]{0:T(128)} %copy-done.7) | copy-start | bytes 388
  648.3 14.0 %copy-start.10 = (s32[32]{0:T(128)S(1)}, s32[32]{0:T(128)}, u32[]{:S(2)}) copy-start(s32[32]{0:T(128)} %copy-done.9) | copy-start | bytes 388
  648.4 39.1 %collective-permute-start.5 = (bf16[1,2,64,2048]{3,2,1,0:T(8,128)(2,1)S(1)}, bf16[1,2,64,2048]{3,2,1,0:T(8,128)(2,1)S(1)}, u32[]{:S(2)}, u32[]{:S(2)}) collective-permute-start(bf16[1,2,64,2048]{3,2,1,0:T(8,128)(2,1)S(1)} %pad_maximum_fusion), channel_id=1, source_target_pairs={{0,0},{1,1},{2,2},{3,3},{4,4},{5,5},{6,6},{7,7},{8,8},{9,9},{10,10... | collective-permute-start | bytes 1572872 | tf_op jit(solution)/shard_map/ppermute | solution.py:26
  663.0 11.0 %all-to-all-start.7 = ((bf16[32,1,32]{2,1,0:T(2,128)(2,1)}), bf16[32,1,32]{2,1,0:T(2,128)(2,1)S(1)}, u32[]{:S(2)}, u32[]{:S(2)}) async-start(bf16[32,1,32]{2,1,0:T(2,128)(2,1)} %copy.105), calls=%async_computation.7 | async-start | bytes 32768 | tf_op jit(solution)/shard_map/all_to_all | solution.py:160
  674.0 9.7 %all-to-all-start.6 = ((bf16[32,1,32]{2,1,0:T(2,128)(2,1)}), bf16[32,1,32]{2,1,0:T(2,128)(2,1)S(1)}, u32[]{:S(2)}, u32[]{:S(2)}) async-start(bf16[32,1,32]{2,1,0:T(2,128)(2,1)} %copy.104), calls=%async_computation.6 | async-start | bytes 32768 | tf_op jit(solution)/shard_map/all_to_all | solution.py:160
